TPU v7x, 32 devices: a whole 2x2x4 slice. The times are simulated.
32 devices in a mesh: rows: 16 (over z, y, x), rep: 2 (over core).
Axes of the slice: x: 2, y: 2, z: 4, core: 2. Of those that a mesh axis runs over, the one named last changes fastest.
Arguments:
- grad_out: bfloat16 [2048, 1024], P('rows'), may hold values from -8 to 8
- w_self: bfloat16 [1024, 1024], replicated, may hold values from -0.1875 to 0.1875
- w_neigh: bfloat16 [1024, 1024], replicated, may hold values from -0.1875 to 0.1875
- adj_tiles: bfloat16 [16, 8, 128, 128], P('rows'), may hold values from -0.3125 to 0.3125
- tile_index: int32 [16, 8], P('rows'), may hold values from 0 to 15, as said below
- tile_count: int32 [16], P('rows'), may hold values from 4 to 8, as said below
- prompt_ids: int32 [2048], P('rows'), may hold values from 0 to 15
Outputs:
- input_grad: bfloat16 [2048, 1024], P('rows')
- prompt_grad: float32 [16, 1024], replicated
Inputs may be any that keep to these rules, and one draw needn't show every extreme that they name: `tile_index`: each row holds 8 different tile numbers; only the first tile_count entries of a row are used. `tile_count`: some destination tile uses all 8 slots.
All inputs are finite; a program needn't handle non-finite values.
Results may differ from a plain program's by a relative error of at most 0.0041.
Values may be sent and summed in bfloat16 or wider, within the bound.
A program may use at most 64 MiB of HBM per device.

v0:
```python
import math
import jax
import jax.numpy as jnp
from jax import lax
from jax.sharding import PartitionSpec as P

PROMPTS = 16


def shards(grad_out, w_self, w_neigh, adj_tiles, tile_index, tile_count, prompt_ids):
    rows_dev, width = grad_out.shape
    local_tiles, max_slots, tile_size, _ = adj_tiles.shape
    n_rows = lax.axis_size("rows")
    n_rep = lax.axis_size("rep")
    rep_index = lax.axis_index("rep")
    total_tiles = local_tiles * n_rows
    slot_ids = jnp.arange(max_slots)
    in_use = slot_ids[None, :] < tile_count[:, None]
    matches = (tile_index[:, :, None] == jnp.arange(total_tiles)[None, None, :]) & in_use[
        :, :, None
    ]
    present = jnp.any(matches, axis=1)
    slot_table = jnp.argmax(matches, axis=1)
    contract = (((1,), (1,)), ((), ()))
    half_rows = rows_dev // n_rep
    mine = lax.dynamic_slice_in_dim(grad_out, rep_index * half_rows, half_rows, 0)
    initial = jnp.zeros((local_tiles, tile_size, width), jnp.float32)

    def half_column(place):
        return place // half_rows * rows_dev + rep_index * half_rows + place % half_rows

    piece = lax.all_gather(mine, "rows", axis=0, tiled=True)
    piece_rows = piece.shape[0]
    unit = math.gcd(math.gcd(piece_rows, tile_size), half_rows)
    segments = piece_rows // unit
    feat = piece.shape[1]

    def one_segment(index, carry):
        start = index * unit
        rows_part = lax.dynamic_slice_in_dim(piece, start, unit, 0)
        column = half_column(start)
        source = column // tile_size
        offset = column % tile_size
        slot = slot_table[0, source]
        zero = jnp.zeros((), jnp.int32)
        block = lax.dynamic_slice(
            adj_tiles, (jnp.int32(0), slot, zero, offset), (1, 1, tile_size, unit)
        )
        block = block.reshape(tile_size, unit)

        def product(args):
            blk, part_rows = args
            return jnp.dot(blk, part_rows, preferred_element_type=jnp.float32)

        def nothing(args):
            return jnp.zeros((tile_size, feat), jnp.float32)

        term = lax.cond(present[0, source], product, nothing, (block, rows_part))
        updated = [carry[0] + term]
        return jnp.stack(updated, axis=0)

    partial_value = lax.fori_loop(0, segments, one_segment, initial)
    summed = lax.psum(partial_value.reshape(rows_dev, width), "rep")
    aggregate = summed.astype(jnp.bfloat16)
    full_grad = lax.dot_general(grad_out, w_self, contract, preferred_element_type=jnp.float32)
    full_grad = full_grad + lax.dot_general(
        aggregate, w_neigh, contract, preferred_element_type=jnp.float32
    )
    onehot = (prompt_ids[None, :] == jnp.arange(PROMPTS)[:, None]).astype(jnp.float32)
    prompt_part = jnp.dot(onehot, full_grad, precision=lax.Precision.HIGHEST)
    prompt_grad = lax.psum(prompt_part, "rows")
    return (full_grad.astype(jnp.bfloat16), prompt_grad)


def solution(mesh):
    placed = (
        P("rows", None),
        P(),
        P(),
        P("rows", None, None, None),
        P("rows", None),
        P("rows"),
        P("rows"),
    )
    return jax.shard_map(
        shards, mesh=mesh, in_specs=placed, out_specs=(P("rows", None), P()), check_vma=False
    )
```

profile of v0, /device:TPU:0, one launch (start us, length us, event | category | flops | bytes accessed | tf_op | source)
XLA Modules:
  0.0 249.7 jit_solution(9167569189331557641)
XLA Ops:
  7.2 1.7 constant_dynamic-slice_fusion.2
  10.4 1.3 iota_reduce_fusion
  11.7 3.3 %fusion.13 = f32[128,1024]{1,0:T(8,128)} fusion(bf16[128,1024]{1,0:T(8,128)(2,1)} %param.11, bf16[1024,1024]{1,0:T(8,128)(2,1)} %param.12), kind=kOutput, calls=%fused_computation.22 | convolution fusion | flops 268435456 | bytes 2883584 | tf_op jit(solution)/shard_map/dot_general | solution.py:65
  15.0 59.5 %all-gather.2.cloned.1.call-done = bf16[1024,1024]{1,0:T(8,128)(2,1)} async-done(((bf16[64,1024]{1,0:T(8,128)(2,1)}), bf16[1024,1024]{1,0:T(8,128)(2,1)}) %all-gather.2.cloned.1.call-update) | async-done | bytes 2097168 | tf_op jit(solution)/shard_map/all_gather | solution.py:32
  74.5 45.9 %while.16 = (s32[]{:T(128)}, f32[1,128,1024]{2,1,0:T(8,128)S(1)}, s32[]{:T(128)}, pred[1,16]{1,0:T(4,128)(4,1)S(1)}, s32[1,16]{1,0:T(1,128)S(1)}, /*index=5*/bf1...) while((s32[]{:T(128)}, f32[1,128,1024]{2,1,0:T(8,128)S(1)}, ...), condition=%wide.region_5.6_spmd, body=%wide.region_2.5_spmd.sunk | while | flops 16908344 | bytes 2261804 | solution.py:62
  75.3 4.7 %conditional.2 = (f32[128,1024]{1,0:T(8,128)S(1)}) conditional(s32[]{:T(128)} %bitcast.25, () %tuple.66, (s32[1,16]{1,0:T(1,128)S(1)}, s32[]{:T(128)}, s32[]{:T(128)}, bf16[1,8,128,128]{3,2,1,0:T(8,128)(2,1)}, s32[]{:T(128)}, /*index=5*/pred[]{:T(512)}, bf16[1024,1024]{1,0:T(8,128)(2,1)}) %tuple.67), branch_computations={%region_3.3_spmd, %region_4.4_spmd} | conditional | flops 16777228 | bytes 688299 | solution.py:58
  78.7 1.2 fusion
  80.8 4.7 %conditional.2 = (f32[128,1024]{1,0:T(8,128)S(1)}) conditional(s32[]{:T(128)} %bitcast.25, () %tuple.66, (s32[1,16]{1,0:T(1,128)S(1)}, s32[]{:T(128)}, s32[]{:T(128)}, bf16[1,8,128,128]{3,2,1,0:T(8,128)(2,1)}, s32[]{:T(128)}, /*index=5*/pred[]{:T(512)}, bf16[1024,1024]{1,0:T(8,128)(2,1)}) %tuple.67), branch_computations={%region_3.3_spmd, %region_4.4_spmd} | conditional | flops 16777228 | bytes 688299 | solution.py:58
  84.3 1.2 fusion
  86.4 0.8 conditional.2
  88.0 0.8 conditional.2
  89.7 0.8 conditional.2
  91.3 4.7 %conditional.2 = (f32[128,1024]{1,0:T(8,128)S(1)}) conditional(s32[]{:T(128)} %bitcast.25, () %tuple.66, (s32[1,16]{1,0:T(1,128)S(1)}, s32[]{:T(128)}, s32[]{:T(128)}, bf16[1,8,128,128]{3,2,1,0:T(8,128)(2,1)}, s32[]{:T(128)}, /*index=5*/pred[]{:T(512)}, bf16[1024,1024]{1,0:T(8,128)(2,1)}) %tuple.67), branch_computations={%region_3.3_spmd, %region_4.4_spmd} | conditional | flops 16777228 | bytes 688299 | solution.py:58
  94.8 1.2 fusion
  96.9 4.7 %conditional.2 = (f32[128,1024]{1,0:T(8,128)S(1)}) conditional(s32[]{:T(128)} %bitcast.25, () %tuple.66, (s32[1,16]{1,0:T(1,128)S(1)}, s32[]{:T(128)}, s32[]{:T(128)}, bf16[1,8,128,128]{3,2,1,0:T(8,128)(2,1)}, s32[]{:T(128)}, /*index=5*/pred[]{:T(512)}, bf16[1024,1024]{1,0:T(8,128)(2,1)}) %tuple.67), branch_computations={%region_3.3_spmd, %region_4.4_spmd} | conditional | flops 16777228 | bytes 688299 | solution.py:58
  100.3 1.2 fusion
  107.3 4.7 %conditional.2 = (f32[128,1024]{1,0:T(8,128)S(1)}) conditional(s32[]{:T(128)} %bitcast.25, () %tuple.66, (s32[1,16]{1,0:T(1,128)S(1)}, s32[]{:T(128)}, s32[]{:T(128)}, bf16[1,8,128,128]{3,2,1,0:T(8,128)(2,1)}, s32[]{:T(128)}, /*index=5*/pred[]{:T(512)}, bf16[1024,1024]{1,0:T(8,128)(2,1)}) %tuple.67), branch_computations={%region_3.3_spmd, %region_4.4_spmd} | conditional | flops 16777228 | bytes 688299 | solution.py:58
  110.8 1.2 fusion
  112.9 0.8 conditional.2
  120.4 4.8 %all-reduce.4 = bf16[128,1024]{1,0:T(8,128)(2,1)S(1)} all-reduce(f32[128,1024]{1,0:T(8,128)S(1)} %bitcast.27), channel_id=1, replica_groups=mesh['rows'=16,'rep'=2] {'rep'}, use_global_device_ids=true, to_apply=%region_6.7 | all-reduce | flops 131072 | bytes 786432 | tf_op jit(solution)/shard_map/psum | solution.py:63
  125.2 2.6 %fusion.12 = (bf16[128,1024]{1,0:T(8,128)(2,1)}, f32[128,1024]{1,0:T(8,128)S(1)}) fusion(f32[128,1024]{1,0:T(8,128)} %fusion.13, bf16[128,1024]{1,0:T(8,128)(2,1)S(1)} %all-reduce.4, bf16[1024,1024]{1,0:T(8,128)(2,1)S(1)} %copy-done), kind=kOutput, calls=%fused_computation.21 | convolution fusion | flops 268697600 | bytes 3670016 | tf_op jit(solution)/shard_map/dot_general | solution.py:66
  127.8 0.9 fusion.7
  128.8 112.6 %all-reduce.3.cloned.1.call-done = f32[16,1024]{1,0:T(8,128)} async-done(((f32[16,1024]{1,0:T(8,128)}), f32[16,1024]{1,0:T(8,128)}) %all-reduce.3.cloned.1.call-update) | async-done | bytes 65552 | tf_op jit(solution)/shard_map/psum | solution.py:71
  241.4 1.5 copy.21
  (66 shorter events, 22.8 us)
Async XLA Ops:
  7.2 118.1 %copy-start = (bf16[1024,1024]{1,0:T(8,128)(2,1)S(1)}, bf16[1024,1024]{1,0:T(8,128)(2,1)}, u32[]{:S(2)}) copy-start(bf16[1024,1024]{1,0:T(8,128)(2,1)} %param.13) | copy-start | bytes 6291460
  7.2 67.3 %all-gather.2.cloned.1.call-start = ((), (), s32[]{:S(2)}) async-start(), calls=%async_computation | async-start | bytes 2228224 | tf_op jit(solution)/shard_map/all_gather | solution.py:32
  9.0 232.4 %all-reduce.3.cloned.1.call-start = ((), (), s32[]{:S(2)}) async-start(), calls=%async_computation.1 | async-start | bytes 131072 | tf_op jit(solution)/shard_map/psum | solution.py:71
  120.4 7.4 %copy-start.1 = (s32[128]{0:T(128)S(1)}, s32[128]{0:T(128)}, u32[]{:S(2)}) copy-start(s32[128]{0:T(128)} %param.17) | copy-start | bytes 1540
Sparse Core Ops, SparseCore 0:
  11.3 63.0 all-gather.1
  128.9 112.4 all-reduce.2
where the time goes:
time: 250 us
  waiting for transfers between devices  172 us (69%)
  loops' own time  23.3 us (9%)
  other arithmetic  14.8 us (6%)
  between operations  14.7 us (6%)
  matrix products  12.8 us (5%)
  local copies, waits for them, and re-layouts  7.06 us (3%)
  blocking collectives  4.82 us (2%)
    psum x1, waiting for transfers between devices, shards(): prompt_grad = lax.psum(prompt_part, 'rows')  113 us
    all_gather x1, waiting for transfers between devices, shards(): piece = lax.all_gather(mine, 'rows', axis=0, tiled=True)  59.5 us
    another operation x16, loops' own time, one_segment(): term = lax.cond(present[0, source], product, nothing, (block, rows_part))  21.9 us
    convert_element_type x16, other arithmetic, one_segment(): term = lax.cond(present[0, source], product, nothing, (block, rows_part))  10.6 us
    dot_general x5, matrix products, product(): return jnp.dot(blk, part_rows, preferred_element_type=jnp.float32)  5.96 us
  transfers between devices with their start and end apart: 2, of which 2 were waited for; matrix products, arithmetic and copies ran while one was open for 2% of the time, Pallas kernels for 0%

commit v1 on v0

--- a/solution.py
+++ b/solution.py
@@ -68,7 +68,11 @@
     )
     onehot = (prompt_ids[None, :] == jnp.arange(PROMPTS)[:, None]).astype(jnp.float32)
     prompt_part = jnp.dot(onehot, full_grad, precision=lax.Precision.HIGHEST)
-    prompt_grad = lax.psum(prompt_part, "rows")
+    prompt_grad = prompt_part
+    for hop in (1, 2, 4, 8):
+        prompt_grad = prompt_grad + lax.ppermute(
+            prompt_grad, "rows", [(dev, dev ^ hop) for dev in range(16)]
+        )
     return (full_grad.astype(jnp.bfloat16), prompt_grad)
 
 

time: 250 us -> 165 us (0.66)
  waiting for transfers between devices: 172 us -> 75.7 us
  starting transfers between devices: 0.08 us -> 12.3 us
    psum x1 -> x0, waiting for transfers between devices: 113 us -> none  [shards(): prompt_grad = lax.psum(prompt_part, 'rows')]
    ppermute x0 -> x4, waiting for transfers between devices: none -> 16.1 us  [shards(): lax.ppermute(prompt_grad, 'rows', [(dev, dev ^ hop) for dev in range(16)])]
    ppermute x0 -> x4, starting transfers between devices: none -> 12.3 us  [shards(): lax.ppermute(prompt_grad, 'rows', [(dev, dev ^ hop) for dev in range(16)])]
  transfers between devices with their start and end apart: 2 -> 5, of which waited for: 2 -> 5; matrix products, arithmetic and copies ran while one was open for 2% -> 3% of each run, Pallas kernels for 0% -> 0%
where the time goes in v1:
time: 165 us; the launch traced here: 164 us
  waiting for transfers between devices  75.7 us (46%)
  loops' own time  23.3 us (14%)
  other arithmetic  15.4 us (9%)
  between operations  14.8 us (9%)
  starting transfers between devices  12.3 us (7%)
  matrix products  12.2 us (7%)
  local copies, waits for them, and re-layouts  5.59 us (3%)
  blocking collectives  4.82 us (3%)
    all_gather x1, waiting for transfers between devices, shards(): piece = lax.all_gather(mine, 'rows', axis=0, tiled=True)  59.5 us
    another operation x16, loops' own time, one_segment(): term = lax.cond(present[0, source], product, nothing, (block, rows_part))  21.9 us
    ppermute x4, waiting for transfers between devices, shards(): lax.ppermute(prompt_grad, 'rows', [(dev, dev ^ hop) for dev in range(16)])  16.1 us
    ppermute x4, starting transfers between devices, shards(): lax.ppermute(prompt_grad, 'rows', [(dev, dev ^ hop) for dev in range(16)])  12.3 us
    convert_element_type x16, other arithmetic, one_segment(): term = lax.cond(present[0, source], product, nothing, (block, rows_part))  10.6 us
    dot_general x5, matrix products, product(): return jnp.dot(blk, part_rows, preferred_element_type=jnp.float32)  5.96 us
    psum x1, blocking collectives, shards(): summed = lax.psum(partial_value.reshape(rows_dev, width), 'rep')  4.82 us
    dynamic_slice x5, local copies, waits for them, and re-layouts, one_segment(): slot = slot_table[0, source]  3.34 us
  transfers between devices with their start and end apart: 5, of which 5 were waited for; matrix products, arithmetic and copies ran while one was open for 3% of the time, Pallas kernels for 0%

profile of v1, /device:TPU:0, one launch (start us, length us, event | category | flops | bytes accessed | tf_op | source)
XLA Modules:
  0.0 164.1 jit_solution(10900259326293556968)
XLA Ops:
  7.2 1.7 %constant_dynamic-slice_fusion.2 = bf16[64,1024]{1,0:T(8,128)(2,1)} fusion(bf16[128,1024]{1,0:T(8,128)(2,1)} %param.11, s32[]{:T(128)S(6)} %select_n.120), kind=kLoop, calls=%fused_computation.19 | loop fusion | bytes 262148 | tf_op jit(solution)/shard_map/dynamic_slice | solution.py:26
  10.4 1.3 iota_reduce_fusion
  11.6 3.3 %fusion.13 = f32[128,1024]{1,0:T(8,128)} fusion(bf16[128,1024]{1,0:T(8,128)(2,1)} %param.11, bf16[1024,1024]{1,0:T(8,128)(2,1)} %param.12), kind=kOutput, calls=%fused_computation.22 | convolution fusion | flops 268435456 | bytes 2883584 | tf_op jit(solution)/shard_map/dot_general | solution.py:65
  15.0 59.5 %all-gather.2.cloned.1.call-done = bf16[1024,1024]{1,0:T(8,128)(2,1)} async-done(((bf16[64,1024]{1,0:T(8,128)(2,1)}), bf16[1024,1024]{1,0:T(8,128)(2,1)}) %all-gather.2.cloned.1.call-update) | async-done | bytes 2097168 | tf_op jit(solution)/shard_map/all_gather | solution.py:32
  74.5 45.9 %while.16 = (s32[]{:T(128)}, f32[1,128,1024]{2,1,0:T(8,128)S(1)}, s32[]{:T(128)}, pred[1,16]{1,0:T(4,128)(4,1)S(1)}, s32[1,16]{1,0:T(1,128)S(1)}, /*index=5*/bf1...) while((s32[]{:T(128)}, f32[1,128,1024]{2,1,0:T(8,128)S(1)}, ...), condition=%wide.region_5.6_spmd, body=%wide.region_2.5_spmd.sunk | while | flops 16908344 | bytes 2261804 | solution.py:62
  75.3 4.7 %conditional.2 = (f32[128,1024]{1,0:T(8,128)S(1)}) conditional(s32[]{:T(128)} %bitcast.25, () %tuple.66, (s32[1,16]{1,0:T(1,128)S(1)}, s32[]{:T(128)}, s32[]{:T(128)}, bf16[1,8,128,128]{3,2,1,0:T(8,128)(2,1)}, s32[]{:T(128)}, /*index=5*/pred[]{:T(512)}, bf16[1024,1024]{1,0:T(8,128)(2,1)}) %tuple.67), branch_computations={%region_3.3_spmd, %region_4.4_spmd} | conditional | flops 16777228 | bytes 688299 | solution.py:58
  78.7 1.2 fusion
  80.8 4.7 %conditional.2 = (f32[128,1024]{1,0:T(8,128)S(1)}) conditional(s32[]{:T(128)} %bitcast.25, () %tuple.66, (s32[1,16]{1,0:T(1,128)S(1)}, s32[]{:T(128)}, s32[]{:T(128)}, bf16[1,8,128,128]{3,2,1,0:T(8,128)(2,1)}, s32[]{:T(128)}, /*index=5*/pred[]{:T(512)}, bf16[1024,1024]{1,0:T(8,128)(2,1)}) %tuple.67), branch_computations={%region_3.3_spmd, %region_4.4_spmd} | conditional | flops 16777228 | bytes 688299 | solution.py:58
  84.3 1.2 fusion
  88.0 0.8 conditional.2
  89.7 0.8 conditional.2
  91.3 4.7 %conditional.2 = (f32[128,1024]{1,0:T(8,128)S(1)}) conditional(s32[]{:T(128)} %bitcast.25, () %tuple.66, (s32[1,16]{1,0:T(1,128)S(1)}, s32[]{:T(128)}, s32[]{:T(128)}, bf16[1,8,128,128]{3,2,1,0:T(8,128)(2,1)}, s32[]{:T(128)}, /*index=5*/pred[]{:T(512)}, bf16[1024,1024]{1,0:T(8,128)(2,1)}) %tuple.67), branch_computations={%region_3.3_spmd, %region_4.4_spmd} | conditional | flops 16777228 | bytes 688299 | solution.py:58
  94.8 1.2 fusion
  96.9 4.7 %conditional.2 = (f32[128,1024]{1,0:T(8,128)S(1)}) conditional(s32[]{:T(128)} %bitcast.25, () %tuple.66, (s32[1,16]{1,0:T(1,128)S(1)}, s32[]{:T(128)}, s32[]{:T(128)}, bf16[1,8,128,128]{3,2,1,0:T(8,128)(2,1)}, s32[]{:T(128)}, /*index=5*/pred[]{:T(512)}, bf16[1024,1024]{1,0:T(8,128)(2,1)}) %tuple.67), branch_computations={%region_3.3_spmd, %region_4.4_spmd} | conditional | flops 16777228 | bytes 688299 | solution.py:58
  100.3 1.2 fusion
  107.3 4.7 %conditional.2 = (f32[128,1024]{1,0:T(8,128)S(1)}) conditional(s32[]{:T(128)} %bitcast.25, () %tuple.66, (s32[1,16]{1,0:T(1,128)S(1)}, s32[]{:T(128)}, s32[]{:T(128)}, bf16[1,8,128,128]{3,2,1,0:T(8,128)(2,1)}, s32[]{:T(128)}, /*index=5*/pred[]{:T(512)}, bf16[1024,1024]{1,0:T(8,128)(2,1)}) %tuple.67), branch_computations={%region_3.3_spmd, %region_4.4_spmd} | conditional | flops 16777228 | bytes 688299 | solution.py:58
  110.8 1.2 fusion
  120.4 4.8 %all-reduce.1 = bf16[128,1024]{1,0:T(8,128)(2,1)S(1)} all-reduce(f32[128,1024]{1,0:T(8,128)S(1)} %bitcast.27), channel_id=1, replica_groups=mesh['rows'=16,'rep'=2] {'rep'}, use_global_device_ids=true, to_apply=%region_6.7 | all-reduce | flops 131072 | bytes 786432 | tf_op jit(solution)/shard_map/psum | solution.py:63
  125.2 2.6 %fusion.12 = (bf16[128,1024]{1,0:T(8,128)(2,1)}, f32[128,1024]{1,0:T(8,128)S(1)}) fusion(f32[128,1024]{1,0:T(8,128)} %fusion.13, bf16[128,1024]{1,0:T(8,128)(2,1)S(1)} %all-reduce.1, bf16[1024,1024]{1,0:T(8,128)(2,1)S(1)} %copy-done), kind=kOutput, calls=%fused_computation.21 | convolution fusion | flops 268697600 | bytes 3670016 | tf_op jit(solution)/shard_map/dot_general | solution.py:66
  128.2 4.4 %collective-permute-done = f32[16,1024]{1,0:T(8,128)S(1)} collective-permute-done((f32[16,1024]{1,0:T(8,128)S(1)}, f32[16,1024]{1,0:T(8,128)S(1)}, u32[]{:S(2)}, u32[]{:S(2)}) %collective-permute-start) | collective-permute-done | bytes 65568 | tf_op jit(solution)/shard_map/ppermute | solution.py:73
  132.6 12.1 %collective-permute-start.1 = (f32[16,1024]{1,0:T(8,128)S(1)}, f32[16,1024]{1,0:T(8,128)S(1)}, u32[]{:S(2)}, u32[]{:S(2)}) collective-permute-start(f32[16,1024]{1,0:T(8,128)S(1)} %add.160), channel_id=1, source_target_pairs={{0,4},{2,6},{4,0},{6,2},{8,12},{10,14},{12,8},{14,10},{16,20},{18,... | collective-permute-start | bytes 196616 | tf_op jit(solution)/shard_map/ppermute | solution.py:73
  144.7 2.2 %collective-permute-done.1 = f32[16,1024]{1,0:T(8,128)S(1)} collective-permute-done((f32[16,1024]{1,0:T(8,128)S(1)}, f32[16,1024]{1,0:T(8,128)S(1)}, u32[]{:S(2)}, u32[]{:S(2)}) %collective-permute-start.1) | collective-permute-done | bytes 65568 | tf_op jit(solution)/shard_map/ppermute | solution.py:73
  147.0 4.3 %collective-permute-done.2 = f32[16,1024]{1,0:T(8,128)S(1)} collective-permute-done((f32[16,1024]{1,0:T(8,128)S(1)}, f32[16,1024]{1,0:T(8,128)S(1)}, u32[]{:S(2)}, u32[]{:S(2)}) %collective-permute-start.2) | collective-permute-done | bytes 65568 | tf_op jit(solution)/shard_map/ppermute | solution.py:73
  151.3 5.3 %collective-permute-done.3 = f32[16,1024]{1,0:T(8,128)S(1)} collective-permute-done((f32[16,1024]{1,0:T(8,128)S(1)}, f32[16,1024]{1,0:T(8,128)S(1)}, u32[]{:S(2)}, u32[]{:S(2)}) %collective-permute-start.3) | collective-permute-done | bytes 65568 | tf_op jit(solution)/shard_map/ppermute | solution.py:73
  (74 shorter events, 25.4 us)
Async XLA Ops:
  7.2 118.1 %copy-start = (bf16[1024,1024]{1,0:T(8,128)(2,1)S(1)}, bf16[1024,1024]{1,0:T(8,128)(2,1)}, u32[]{:S(2)}) copy-start(bf16[1024,1024]{1,0:T(8,128)(2,1)} %param.13) | copy-start | bytes 6291460
  7.2 67.3 %all-gather.2.cloned.1.call-start = ((), (), s32[]{:S(2)}) async-start(), calls=%async_computation | async-start | bytes 2228224 | tf_op jit(solution)/shard_map/all_gather | solution.py:32
  120.4 7.4 %copy-start.1 = (s32[128]{0:T(128)S(1)}, s32[128]{0:T(128)}, u32[]{:S(2)}) copy-start(s32[128]{0:T(128)} %param.17) | copy-start | bytes 1540
  128.1 4.4 %collective-permute-start = (f32[16,1024]{1,0:T(8,128)S(1)}, f32[16,1024]{1,0:T(8,128)S(1)}, u32[]{:S(2)}, u32[]{:S(2)}) collective-permute-start(f32[16,1024]{1,0:T(8,128)S(1)} %fusion.7), channel_id=1, source_target_pairs={{0,2},{2,0},{4,6},{6,4},{8,10},{10,8},{12,14},{14,12},{16,18},{18,... | collective-permute-start | bytes 196616 | tf_op jit(solution)/shard_map/ppermute | solution.py:73
  132.6 14.3 %collective-permute-start.1 = (f32[16,1024]{1,0:T(8,128)S(1)}, f32[16,1024]{1,0:T(8,128)S(1)}, u32[]{:S(2)}, u32[]{:S(2)}) collective-permute-start(f32[16,1024]{1,0:T(8,128)S(1)} %add.160), channel_id=1, source_target_pairs={{0,4},{2,6},{4,0},{6,2},{8,12},{10,14},{12,8},{14,10},{16,20},{18,... | collective-permute-start | bytes 196616 | tf_op jit(solution)/shard_map/ppermute | solution.py:73
  146.9 4.3 %collective-permute-start.2 = (f32[16,1024]{1,0:T(8,128)S(1)}, f32[16,1024]{1,0:T(8,128)S(1)}, u32[]{:S(2)}, u32[]{:S(2)}) collective-permute-start(f32[16,1024]{1,0:T(8,128)S(1)} %add.161), channel_id=1, source_target_pairs={{0,8},{2,10},{4,12},{6,14},{8,0},{10,2},{12,4},{14,6},{16,24},{18,... | collective-permute-start | bytes 196616 | tf_op jit(solution)/shard_map/ppermute | solution.py:73
  151.3 5.4 %collective-permute-start.3 = (f32[16,1024]{1,0:T(8,128)S(1)}, f32[16,1024]{1,0:T(8,128)S(1)}, u32[]{:S(2)}, u32[]{:S(2)}) collective-permute-start(f32[16,1024]{1,0:T(8,128)S(1)} %add.162), channel_id=1, source_target_pairs={{0,16},{2,18},{4,20},{6,22},{8,24},{10,26},{12,28},{14,30},{16,0},... | collective-permute-start | bytes 196616 | tf_op jit(solution)/shard_map/ppermute | solution.py:73
Sparse Core Ops, SparseCore 0:
  11.3 63.0 all-gather.1
